TPU v7x, 512 devices: a whole 4x4x16 slice. The times are simulated.
512 devices in a mesh: grp: 16 (over z), row: 32 (over x, y, core).
Axes of the slice: x: 4, y: 4, z: 16, core: 2. Of those that a mesh axis runs over, the one named last changes fastest.
Arguments:
- design: bfloat16 [786432, 512], P(('grp', 'row')), may hold values from -0.29882812 to 0.29882812
- scales: bfloat16 [786432], P(('grp', 'row')), may hold values from 0.3984375 to 9.5
- buckets: int32 [786432], P(('grp', 'row')), may hold values from 0 to 1535
Outputs:
- sketch: float32 [24576, 512], P(('grp', 'row'))
- precond: float32 [512, 512], P('grp')
All inputs are finite; a program needn't handle non-finite values.
Results may differ from a plain program's by a relative error of at most 0.0003.
Values sent between devices are 32-bit elements; how exact they have to be, the bound alone decides.
No kernel may reach another device: no remote copies, remote signals or barrier semaphores. Data moves between devices by JAX's collectives and lax.ppermute only.
A program may use at most 64 MiB of HBM per device.

v0:
```python
import jax
import jax.numpy as jnp
from jax import lax
from jax.sharding import PartitionSpec as P


def partner_2(block, axis, stride):
    count = lax.axis_size(axis)
    route = []
    for low in range(count):
        high = low | 1 << stride
        if high != low and high < count:
            route += [(low, high), (high, low)]
    return lax.ppermute(block, axis, route)


def chol_upper(gram_matrix):
    return jnp.linalg.cholesky(gram_matrix).T


def self_gram(matrix):
    return lax.dot_general(
        matrix,
        matrix,
        (((0,), (0,)), ((), ())),
        precision=lax.Precision.HIGHEST,
        preferred_element_type=jnp.float32,
    )


def per_device(design, scales, buckets):
    row_count = design.shape[0]
    col_count = design.shape[1]
    row_parts = lax.axis_size("row")
    owned_rows = row_count // row_parts
    label_ids = lax.iota(jnp.int32, row_count)
    onehot_table = jnp.where(
        label_ids[:, None] == buckets[None, :], scales[None, :], jnp.zeros((), jnp.bfloat16)
    )
    partial_value = jnp.dot(onehot_table, design, preferred_element_type=jnp.float32).reshape(
        row_parts, owned_rows, col_count
    )
    arrived = lax.all_to_all(partial_value, "row", split_axis=0, concat_axis=0, tiled=True)
    sketch = jnp.sum(arrived, axis=0)
    local_gram = self_gram(sketch)
    group_gram = lax.psum(local_gram, "row")
    factor = chol_upper(group_gram)
    for bit_index in range(lax.axis_size("grp").bit_length() - 1):
        partner = partner_2(factor, "grp", bit_index)
        factor = chol_upper(self_gram(factor) + self_gram(partner))
    precond = factor / jnp.sqrt(jnp.float32(row_count * lax.axis_size("grp")))
    slab_rows = col_count // lax.axis_size("grp")
    slab_start = lax.axis_index("grp") * slab_rows
    precond_rows = lax.dynamic_slice_in_dim(precond, slab_start, slab_rows, 0)
    return (sketch, precond_rows)


def solution(mesh):
    in_specs = (P(("grp", "row"), None), P(("grp", "row")), P(("grp", "row")))
    out_specs = (P(("grp", "row"), None), P("grp", None))
    return jax.shard_map(
        per_device, mesh=mesh, in_specs=in_specs, out_specs=out_specs, check_vma=False
    )
```

profile of v0, /device:TPU:1, one launch (start us, length us, event | category | flops | bytes accessed | tf_op | source)
XLA Modules:
  0.0 933.6 jit_solution(3870824916542653050)
XLA Ops:
  11.9 49.7 %all_to_all.5 = f32[32,48,512]{2,1,0:T(8,128)} all-to-all(f32[32,48,512]{2,1,0:T(8,128)S(1)} %bitcast.130), channel_id=1, replica_groups=mesh['grp'=16,'row'=32] {'row'}, dimensions={0} | all-to-all | bytes 6291456 | tf_op jit(solution)/shard_map/all_to_all | solution.py:43
  65.8 134.5 %all-reduce.3.cloned.1.call-done = f32[512,512]{0,1:T(8,128)} async-done(((f32[512,512]{0,1:T(8,128)}), f32[512,512]{0,1:T(8,128)}) %all-reduce.3.cloned.1.call-update) | async-done | bytes 1048592 | tf_op jit(solution)/shard_map/psum | solution.py:46
  204.4 11.7 %cholesky.550 = f32[128,128]{1,0:T(8,128)S(1)} custom-call(f32[128,128]{1,0:T(8,128)S(1)} %cholesky.906), custom_call_target="Cholesky" | custom-call | tf_op jit(solution)/shard_map/jit(cholesky)/cholesky | solution.py:18
  228.6 12.1 %cholesky.569 = f32[128,128]{1,0:T(8,128)S(1)} custom-call(f32[128,128]{1,0:T(8,128)S(1)} %cholesky.910), custom_call_target="Cholesky" | custom-call | tf_op jit(solution)/shard_map/jit(cholesky)/cholesky | solution.py:18
  252.1 11.7 %cholesky.590 = f32[128,128]{1,0:T(8,128)S(1)} custom-call(f32[128,128]{1,0:T(8,128)S(1)} %cholesky.915), custom_call_target="Cholesky" | custom-call | tf_op jit(solution)/shard_map/jit(cholesky)/cholesky | solution.py:18
  275.8 11.9 %cholesky.607 = f32[128,128]{1,0:T(8,128)S(1)} custom-call(f32[128,128]{1,0:T(8,128)S(1)} %convolution_subtract_fusion.2), custom_call_target="Cholesky" | custom-call | tf_op jit(solution)/shard_map/jit(cholesky)/cholesky | solution.py:18
  296.9 20.7 %collective-permute-done = f32[512,512]{0,1:T(8,128)S(1)} collective-permute-done((f32[512,512]{0,1:T(8,128)S(1)}, f32[512,512]{0,1:T(8,128)S(1)}, u32[]{:S(2)}, u32[]{:S(2)}) %collective-permute-start) | collective-permute-done | bytes 1048608 | tf_op jit(solution)/shard_map/ppermute | solution.py:14
  323.2 11.7 %cholesky.622 = f32[128,128]{1,0:T(8,128)S(1)} custom-call(f32[128,128]{1,0:T(8,128)S(1)} %cholesky.919), custom_call_target="Cholesky" | custom-call | tf_op jit(solution)/shard_map/jit(cholesky)/cholesky | solution.py:18
  347.5 12.1 %cholesky.641 = f32[128,128]{1,0:T(8,128)S(1)} custom-call(f32[128,128]{1,0:T(8,128)S(1)} %cholesky.923), custom_call_target="Cholesky" | custom-call | tf_op jit(solution)/shard_map/jit(cholesky)/cholesky | solution.py:18
  372.3 11.7 %cholesky.662 = f32[128,128]{1,0:T(8,128)S(1)} custom-call(f32[128,128]{1,0:T(8,128)S(1)} %cholesky.928), custom_call_target="Cholesky" | custom-call | tf_op jit(solution)/shard_map/jit(cholesky)/cholesky | solution.py:18
  396.1 11.7 %cholesky.679 = f32[128,128]{1,0:T(8,128)S(1)} custom-call(f32[128,128]{1,0:T(8,128)S(1)} %slice_subtract_fusion.11), custom_call_target="Cholesky" | custom-call | tf_op jit(solution)/shard_map/jit(cholesky)/cholesky | solution.py:18
  417.4 43.2 %collective-permute-done.1 = f32[512,512]{0,1:T(8,128)S(1)} collective-permute-done((f32[512,512]{0,1:T(8,128)S(1)}, f32[512,512]{0,1:T(8,128)S(1)}, u32[]{:S(2)}, u32[]{:S(2)}) %collective-permute-start.1) | collective-permute-done | bytes 1048608 | tf_op jit(solution)/shard_map/ppermute | solution.py:14
  466.3 11.7 %cholesky.694 = f32[128,128]{1,0:T(8,128)S(1)} custom-call(f32[128,128]{1,0:T(8,128)S(1)} %cholesky.932), custom_call_target="Cholesky" | custom-call | tf_op jit(solution)/shard_map/jit(cholesky)/cholesky | solution.py:18
  490.5 12.1 %cholesky.713 = f32[128,128]{1,0:T(8,128)S(1)} custom-call(f32[128,128]{1,0:T(8,128)S(1)} %cholesky.936), custom_call_target="Cholesky" | custom-call | tf_op jit(solution)/shard_map/jit(cholesky)/cholesky | solution.py:18
  515.4 11.7 %cholesky.734 = f32[128,128]{1,0:T(8,128)S(1)} custom-call(f32[128,128]{1,0:T(8,128)S(1)} %cholesky.941), custom_call_target="Cholesky" | custom-call | tf_op jit(solution)/shard_map/jit(cholesky)/cholesky | solution.py:18
  539.2 11.7 %cholesky.751 = f32[128,128]{1,0:T(8,128)S(1)} custom-call(f32[128,128]{1,0:T(8,128)S(1)} %slice_subtract_fusion.10), custom_call_target="Cholesky" | custom-call | tf_op jit(solution)/shard_map/jit(cholesky)/cholesky | solution.py:18
  563.6 88.1 %collective-permute-done.2 = f32[512,512]{0,1:T(8,128)S(1)} collective-permute-done((f32[512,512]{0,1:T(8,128)S(1)}, f32[512,512]{0,1:T(8,128)S(1)}, u32[]{:S(2)}, u32[]{:S(2)}) %collective-permute-start.2) | collective-permute-done | bytes 1048608 | tf_op jit(solution)/shard_map/ppermute | solution.py:14
  657.4 11.7 %cholesky.766 = f32[128,128]{1,0:T(8,128)S(1)} custom-call(f32[128,128]{1,0:T(8,128)S(1)} %cholesky.945), custom_call_target="Cholesky" | custom-call | tf_op jit(solution)/shard_map/jit(cholesky)/cholesky | solution.py:18
  681.6 12.1 %cholesky.785 = f32[128,128]{1,0:T(8,128)S(1)} custom-call(f32[128,128]{1,0:T(8,128)S(1)} %cholesky.949), custom_call_target="Cholesky" | custom-call | tf_op jit(solution)/shard_map/jit(cholesky)/cholesky | solution.py:18
  706.5 11.7 %cholesky.806 = f32[128,128]{1,0:T(8,128)S(1)} custom-call(f32[128,128]{1,0:T(8,128)S(1)} %cholesky.954), custom_call_target="Cholesky" | custom-call | tf_op jit(solution)/shard_map/jit(cholesky)/cholesky | solution.py:18
  730.3 11.7 %cholesky.823 = f32[128,128]{1,0:T(8,128)S(1)} custom-call(f32[128,128]{1,0:T(8,128)S(1)} %slice_subtract_fusion.9), custom_call_target="Cholesky" | custom-call | tf_op jit(solution)/shard_map/jit(cholesky)/cholesky | solution.py:18
  759.6 70.5 %collective-permute-done.3 = f32[512,512]{0,1:T(8,128)} collective-permute-done((f32[512,512]{0,1:T(8,128)}, f32[512,512]{0,1:T(8,128)}, u32[]{:S(2)}, u32[]{:S(2)}) %collective-permute-start.3) | collective-permute-done | bytes 1048608 | tf_op jit(solution)/shard_map/ppermute | solution.py:14
  837.3 11.7 %cholesky.838 = f32[128,128]{1,0:T(8,128)S(1)} custom-call(f32[128,128]{1,0:T(8,128)S(1)} %cholesky.958), custom_call_target="Cholesky" | custom-call | tf_op jit(solution)/shard_map/jit(cholesky)/cholesky | solution.py:18
  861.9 11.9 %cholesky.857 = f32[128,128]{1,0:T(8,128)S(1)} custom-call(f32[128,128]{1,0:T(8,128)S(1)} %cholesky.962), custom_call_target="Cholesky" | custom-call | tf_op jit(solution)/shard_map/jit(cholesky)/cholesky | solution.py:18
  (156 shorter events, 286.3 us)
Async XLA Ops:
  7.2 1.4 copy-start
  7.2 193.2 %all-reduce.3.cloned.1.call-start = ((), (), s32[]{:S(2)}) async-start(), calls=%async_computation.1 | async-start | bytes 2097152 | tf_op jit(solution)/shard_map/psum | solution.py:46
  63.7 139.6 %copy-start.6 = (f32[48,512]{1,0:T(8,128)}, f32[48,512]{1,0:T(8,128)S(1)}, u32[]{:S(2)}) copy-start(f32[48,512]{1,0:T(8,128)S(1)} %reduce_sum.9) | copy-start | bytes 294916
  203.4 1.0 copy-start.5
  291.8 25.8 %collective-permute-start = (f32[512,512]{0,1:T(8,128)S(1)}, f32[512,512]{0,1:T(8,128)S(1)}, u32[]{:S(2)}, u32[]{:S(2)}) collective-permute-start(f32[512,512]{0,1:T(8,128)S(1)} %fusion.24), channel_id=1, source_target_pairs={{0,32},{32,0},{64,96},{96,64},{128,160},{160,128},{192,224},{224,1... | collective-permute-start | bytes 3145736 | tf_op jit(solution)/shard_map/ppermute | solution.py:14
  322.2 1.0 copy-start.2
  411.3 49.3 %collective-permute-start.1 = (f32[512,512]{0,1:T(8,128)S(1)}, f32[512,512]{0,1:T(8,128)S(1)}, u32[]{:S(2)}, u32[]{:S(2)}) collective-permute-start(f32[512,512]{0,1:T(8,128)S(1)} %fusion.21), channel_id=1, source_target_pairs={{0,64},{64,0},{32,96},{96,32},{128,192},{192,128},{160,224},{224,1... | collective-permute-start | bytes 3145736 | tf_op jit(solution)/shard_map/ppermute | solution.py:14
  465.3 1.0 copy-start.3
  554.4 97.4 %collective-permute-start.2 = (f32[512,512]{0,1:T(8,128)S(1)}, f32[512,512]{0,1:T(8,128)S(1)}, u32[]{:S(2)}, u32[]{:S(2)}) collective-permute-start(f32[512,512]{0,1:T(8,128)S(1)} %fusion.18), channel_id=1, source_target_pairs={{0,128},{128,0},{32,160},{160,32},{64,192},{192,64},{96,224},{224,... | collective-permute-start | bytes 3145736 | tf_op jit(solution)/shard_map/ppermute | solution.py:14
  656.4 1.0 copy-start.4
  746.5 83.6 %collective-permute-start.3 = (f32[512,512]{0,1:T(8,128)}, f32[512,512]{0,1:T(8,128)}, u32[]{:S(2)}, u32[]{:S(2)}) collective-permute-start(f32[512,512]{0,1:T(8,128)} %fusion.15), channel_id=1, source_target_pairs={{0,256},{256,0},{32,288},{288,32},{64,320},{320,64},{96,352},{352,... | collective-permute-start | bytes 3145736 | tf_op jit(solution)/shard_map/ppermute | solution.py:14
  836.3 1.0 copy-start.1
Sparse Core Ops, SparseCore 0:
  65.9 134.3 all-reduce.2
where the time goes:
time: 938 us; the launch traced here: 934 us
  other arithmetic  408 us (43%)
  waiting for transfers between devices  357 us (38%)
  matrix products  50.3 us (5%)
  blocking collectives  49.7 us (5%)
  between operations  28 us (3%)
  starting transfers between devices  25.9 us (3%)
  local copies, waits for them, and re-layouts  14.7 us (2%)
    another operation x74, other arithmetic, chol_upper(): return jnp.linalg.cholesky(gram_matrix).T  397 us
    ppermute x4, waiting for transfers between devices, partner_2(): return lax.ppermute(block, axis, route)  222 us
    psum x1, waiting for transfers between devices, per_device(): group_gram = lax.psum(local_gram, 'row')  135 us
    all_to_all x1, blocking collectives, per_device(): lax.all_to_all(partial_value, 'row', split_axis=0, concat_axis=0, tiled=T...  49.7 us
    another operation x30, matrix products, chol_upper(): return jnp.linalg.cholesky(gram_matrix).T  28.3 us
    ppermute x4, starting transfers between devices, partner_2(): return lax.ppermute(block, axis, route)  25.8 us
  transfers between devices with their start and end apart: 5, of which 5 were waited for; matrix products, arithmetic and copies ran while one was open for 1% of the time, Pallas kernels for 0%

commit v1 on v0

--- a/solution.py
+++ b/solution.py
@@ -2,6 +2,15 @@
 import jax.numpy as jnp
 from jax import lax
 from jax.sharding import PartitionSpec as P
+
+
+def add_in_pairs(block, axis):
+    devices = lax.axis_size(axis)
+    acc, stride = (block, 1)
+    while stride < devices:
+        acc = acc + lax.ppermute(acc, axis, [(i, i ^ stride) for i in range(devices)])
+        stride = 2 * stride
+    return acc
 
 
 def partner_2(block, axis, stride):
@@ -43,7 +52,7 @@
     arrived = lax.all_to_all(partial_value, "row", split_axis=0, concat_axis=0, tiled=True)
     sketch = jnp.sum(arrived, axis=0)
     local_gram = self_gram(sketch)
-    group_gram = lax.psum(local_gram, "row")
+    group_gram = add_in_pairs(local_gram, "row")
     factor = chol_upper(group_gram)
     for bit_index in range(lax.axis_size("grp").bit_length() - 1):
         partner = partner_2(factor, "grp", bit_index)

time: 938 us -> 900 us (0.959)
  waiting for transfers between devices: 357 us -> 319 us
  between operations: 28 us -> 14.8 us
  starting transfers between devices: 25.9 us -> 37.7 us
    psum x1 -> x0, waiting for transfers between devices: 135 us -> none  [per_device(): group_gram = lax.psum(local_gram, 'row')]
    ppermute x0 -> x5, waiting for transfers between devices: none -> 95.7 us  [add_in_pairs(): lax.ppermute(acc, axis, [(i, i ^ stride) for i in range(devices)])]
    ppermute x0 -> x5, starting transfers between devices: none -> 12.3 us  [add_in_pairs(): lax.ppermute(acc, axis, [(i, i ^ stride) for i in range(devices)])]
  transfers between devices with their start and end apart: 5 -> 9, of which waited for: 5 -> 9; matrix products, arithmetic and copies ran while one was open for 1% -> 1% of each run, Pallas kernels for 0% -> 0%
where the time goes in v1:
time: 900 us; the launch traced here: 894 us
  other arithmetic  409 us (45%)
  waiting for transfers between devices  319 us (35%)
  blocking collectives  49.7 us (6%)
  matrix products  49.3 us (5%)
  starting transfers between devices  37.7 us (4%)
  between operations  14.8 us (2%)
  local copies, waits for them, and re-layouts  14.6 us (2%)
    another operation x74, other arithmetic, chol_upper(): return jnp.linalg.cholesky(gram_matrix).T  397 us
    ppermute x4, waiting for transfers between devices, partner_2(): return lax.ppermute(block, axis, route)  223 us
    ppermute x5, waiting for transfers between devices, add_in_pairs(): lax.ppermute(acc, axis, [(i, i ^ stride) for i in range(devices)])  95.7 us
    all_to_all x1, blocking collectives, per_device(): lax.all_to_all(partial_value, 'row', split_axis=0, concat_axis=0, tiled=T...  49.7 us
    another operation x30, matrix products, chol_upper(): return jnp.linalg.cholesky(gram_matrix).T  28.3 us
    ppermute x4, starting transfers between devices, partner_2(): return lax.ppermute(block, axis, route)  25.4 us
  transfers between devices with their start and end apart: 9, of which 9 were waited for; matrix products, arithmetic and copies ran while one was open for 1% of the time, Pallas kernels for 0%

profile of v1, /device:TPU:1, one launch (start us, length us, event | category | flops | bytes accessed | tf_op | source)
XLA Modules:
  0.0 893.8 jit_solution(500390742948371762)
XLA Ops:
  5.4 49.7 %all_to_all.5 = f32[32,48,512]{2,1,0:T(8,128)} all-to-all(f32[32,48,512]{2,1,0:T(8,128)S(1)} %bitcast.130), channel_id=1, replica_groups=mesh['grp'=16,'row'=32] {'row'}, dimensions={0} | all-to-all | bytes 6291456 | tf_op jit(solution)/shard_map/all_to_all | solution.py:52
  64.9 24.6 %collective-permute-done.1 = f32[512,512]{0,1:T(8,128)S(1)} collective-permute-done((f32[512,512]{0,1:T(8,128)S(1)}, f32[512,512]{0,1:T(8,128)S(1)}, u32[]{:S(2)}, u32[]{:S(2)}) %collective-permute-start.1) | collective-permute-done | bytes 1048608 | tf_op jit(solution)/shard_map/ppermute | solution.py:11
  92.7 24.1 %collective-permute-done.2 = f32[512,512]{0,1:T(8,128)S(1)} collective-permute-done((f32[512,512]{0,1:T(8,128)S(1)}, f32[512,512]{0,1:T(8,128)S(1)}, u32[]{:S(2)}, u32[]{:S(2)}) %collective-permute-start.2) | collective-permute-done | bytes 1048608 | tf_op jit(solution)/shard_map/ppermute | solution.py:11
  119.0 22.7 %collective-permute-done.3 = f32[512,512]{0,1:T(8,128)S(1)} collective-permute-done((f32[512,512]{0,1:T(8,128)S(1)}, f32[512,512]{0,1:T(8,128)S(1)}, u32[]{:S(2)}, u32[]{:S(2)}) %collective-permute-start.3) | collective-permute-done | bytes 1048608 | tf_op jit(solution)/shard_map/ppermute | solution.py:11
  145.4 21.8 %collective-permute-done.4 = f32[512,512]{0,1:T(8,128)S(1)} collective-permute-done((f32[512,512]{0,1:T(8,128)S(1)}, f32[512,512]{0,1:T(8,128)S(1)}, u32[]{:S(2)}, u32[]{:S(2)}) %collective-permute-start.4) | collective-permute-done | bytes 1048608 | tf_op jit(solution)/shard_map/ppermute | solution.py:11
  171.2 11.7 %cholesky.550 = f32[128,128]{1,0:T(8,128)S(1)} custom-call(f32[128,128]{1,0:T(8,128)S(1)} %cholesky.906), custom_call_target="Cholesky" | custom-call | tf_op jit(solution)/shard_map/jit(cholesky)/cholesky | solution.py:27
  195.4 11.7 %cholesky.569 = f32[128,128]{1,0:T(8,128)S(1)} custom-call(f32[128,128]{1,0:T(8,128)S(1)} %cholesky.910), custom_call_target="Cholesky" | custom-call | tf_op jit(solution)/shard_map/jit(cholesky)/cholesky | solution.py:27
  218.9 11.7 %cholesky.590 = f32[128,128]{1,0:T(8,128)S(1)} custom-call(f32[128,128]{1,0:T(8,128)S(1)} %cholesky.915), custom_call_target="Cholesky" | custom-call | tf_op jit(solution)/shard_map/jit(cholesky)/cholesky | solution.py:27
  242.7 11.7 %cholesky.607 = f32[128,128]{1,0:T(8,128)S(1)} custom-call(f32[128,128]{1,0:T(8,128)S(1)} %slice_subtract_fusion.14), custom_call_target="Cholesky" | custom-call | tf_op jit(solution)/shard_map/jit(cholesky)/cholesky | solution.py:27
  262.5 19.0 %collective-permute-done.5 = f32[512,512]{0,1:T(8,128)S(1)} collective-permute-done((f32[512,512]{0,1:T(8,128)S(1)}, f32[512,512]{0,1:T(8,128)S(1)}, u32[]{:S(2)}, u32[]{:S(2)}) %collective-permute-start.5) | collective-permute-done | bytes 1048608 | tf_op jit(solution)/shard_map/ppermute | solution.py:23
  287.1 11.7 %cholesky.622 = f32[128,128]{1,0:T(8,128)S(1)} custom-call(f32[128,128]{1,0:T(8,128)S(1)} %cholesky.919), custom_call_target="Cholesky" | custom-call | tf_op jit(solution)/shard_map/jit(cholesky)/cholesky | solution.py:27
  311.4 12.1 %cholesky.641 = f32[128,128]{1,0:T(8,128)S(1)} custom-call(f32[128,128]{1,0:T(8,128)S(1)} %cholesky.923), custom_call_target="Cholesky" | custom-call | tf_op jit(solution)/shard_map/jit(cholesky)/cholesky | solution.py:27
  336.2 11.7 %cholesky.662 = f32[128,128]{1,0:T(8,128)S(1)} custom-call(f32[128,128]{1,0:T(8,128)S(1)} %cholesky.928), custom_call_target="Cholesky" | custom-call | tf_op jit(solution)/shard_map/jit(cholesky)/cholesky | solution.py:27
  360.0 11.7 %cholesky.679 = f32[128,128]{1,0:T(8,128)S(1)} custom-call(f32[128,128]{1,0:T(8,128)S(1)} %slice_subtract_fusion.13), custom_call_target="Cholesky" | custom-call | tf_op jit(solution)/shard_map/jit(cholesky)/cholesky | solution.py:27
  380.6 44.8 %collective-permute-done.6 = f32[512,512]{0,1:T(8,128)S(1)} collective-permute-done((f32[512,512]{0,1:T(8,128)S(1)}, f32[512,512]{0,1:T(8,128)S(1)}, u32[]{:S(2)}, u32[]{:S(2)}) %collective-permute-start.6) | collective-permute-done | bytes 1048608 | tf_op jit(solution)/shard_map/ppermute | solution.py:23
  431.0 11.7 %cholesky.694 = f32[128,128]{1,0:T(8,128)S(1)} custom-call(f32[128,128]{1,0:T(8,128)S(1)} %cholesky.932), custom_call_target="Cholesky" | custom-call | tf_op jit(solution)/shard_map/jit(cholesky)/cholesky | solution.py:27
  455.3 12.1 %cholesky.713 = f32[128,128]{1,0:T(8,128)S(1)} custom-call(f32[128,128]{1,0:T(8,128)S(1)} %cholesky.936), custom_call_target="Cholesky" | custom-call | tf_op jit(solution)/shard_map/jit(cholesky)/cholesky | solution.py:27
  480.1 11.7 %cholesky.734 = f32[128,128]{1,0:T(8,128)S(1)} custom-call(f32[128,128]{1,0:T(8,128)S(1)} %cholesky.941), custom_call_target="Cholesky" | custom-call | tf_op jit(solution)/shard_map/jit(cholesky)/cholesky | solution.py:27
  503.9 11.7 %cholesky.751 = f32[128,128]{1,0:T(8,128)S(1)} custom-call(f32[128,128]{1,0:T(8,128)S(1)} %slice_subtract_fusion.12), custom_call_target="Cholesky" | custom-call | tf_op jit(solution)/shard_map/jit(cholesky)/cholesky | solution.py:27
  528.1 88.3 %collective-permute-done.7 = f32[512,512]{0,1:T(8,128)S(1)} collective-permute-done((f32[512,512]{0,1:T(8,128)S(1)}, f32[512,512]{0,1:T(8,128)S(1)}, u32[]{:S(2)}, u32[]{:S(2)}) %collective-permute-start.7) | collective-permute-done | bytes 1048608 | tf_op jit(solution)/shard_map/ppermute | solution.py:23
  646.3 12.1 %cholesky.785 = f32[128,128]{1,0:T(8,128)S(1)} custom-call(f32[128,128]{1,0:T(8,128)S(1)} %cholesky.949), custom_call_target="Cholesky" | custom-call | tf_op jit(solution)/shard_map/jit(cholesky)/cholesky | solution.py:27
  711.1 12.9 %collective-permute-start.8 = (f32[512,512]{0,1:T(8,128)}, f32[512,512]{0,1:T(8,128)}, u32[]{:S(2)}, u32[]{:S(2)}) collective-permute-start(f32[512,512]{0,1:T(8,128)} %fusion.15), channel_id=1, source_target_pairs={{0,256},{256,0},{32,288},{288,32},{64,320},{320,64},{96,352},{352,... | collective-permute-start | bytes 3145736 | tf_op jit(solution)/shard_map/ppermute | solution.py:23
  726.0 70.9 %collective-permute-done.8 = f32[512,512]{0,1:T(8,128)} collective-permute-done((f32[512,512]{0,1:T(8,128)}, f32[512,512]{0,1:T(8,128)}, u32[]{:S(2)}, u32[]{:S(2)}) %collective-permute-start.8) | collective-permute-done | bytes 1048608 | tf_op jit(solution)/shard_map/ppermute | solution.py:23
  828.8 11.9 %cholesky.857 = f32[128,128]{1,0:T(8,128)S(1)} custom-call(f32[128,128]{1,0:T(8,128)S(1)} %cholesky.962), custom_call_target="Cholesky" | custom-call | tf_op jit(solution)/shard_map/jit(cholesky)/cholesky | solution.py:27
  (168 shorter events, 334.9 us)
Async XLA Ops:
  0.6 1.4 copy-start
  57.2 32.5 %copy-start.6 = (f32[48,512]{1,0:T(8,128)}, f32[48,512]{1,0:T(8,128)S(1)}, u32[]{:S(2)}) copy-start(f32[48,512]{1,0:T(8,128)S(1)} %reduce_sum.9) | copy-start | bytes 294916
  58.2 4.6 collective-permute-start
  63.0 26.5 %collective-permute-start.1 = (f32[512,512]{0,1:T(8,128)S(1)}, f32[512,512]{0,1:T(8,128)S(1)}, u32[]{:S(2)}, u32[]{:S(2)}) collective-permute-start(f32[512,512]{0,1:T(8,128)S(1)} %add.60), channel_id=1, source_target_pairs={{0,2},{1,3},{2,0},{3,1},{4,6},{5,7},{6,4},{7,5},{8,10},{9,11},{10,... | collective-permute-start | bytes 3145736 | tf_op jit(solution)/shard_map/ppermute | solution.py:11
  89.7 27.1 %collective-permute-start.2 = (f32[512,512]{0,1:T(8,128)S(1)}, f32[512,512]{0,1:T(8,128)S(1)}, u32[]{:S(2)}, u32[]{:S(2)}) collective-permute-start(f32[512,512]{0,1:T(8,128)S(1)} %add.61), channel_id=1, source_target_pairs={{0,4},{1,5},{2,6},{3,7},{4,0},{5,1},{6,2},{7,3},{8,12},{9,13},{10,... | collective-permute-start | bytes 3145736 | tf_op jit(solution)/shard_map/ppermute | solution.py:11
  117.0 24.7 %collective-permute-start.3 = (f32[512,512]{0,1:T(8,128)S(1)}, f32[512,512]{0,1:T(8,128)S(1)}, u32[]{:S(2)}, u32[]{:S(2)}) collective-permute-start(f32[512,512]{0,1:T(8,128)S(1)} %add.62), channel_id=1, source_target_pairs={{0,8},{1,9},{2,10},{3,11},{4,12},{5,13},{6,14},{7,15},{8,0},{9,1},... | collective-permute-start | bytes 3145736 | tf_op jit(solution)/shard_map/ppermute | solution.py:11
  141.9 25.3 %collective-permute-start.4 = (f32[512,512]{0,1:T(8,128)S(1)}, f32[512,512]{0,1:T(8,128)S(1)}, u32[]{:S(2)}, u32[]{:S(2)}) collective-permute-start(f32[512,512]{0,1:T(8,128)S(1)} %add.63), channel_id=1, source_target_pairs={{0,16},{1,17},{2,18},{3,19},{4,20},{5,21},{6,22},{7,23},{8,24},{9,... | collective-permute-start | bytes 3145736 | tf_op jit(solution)/shard_map/ppermute | solution.py:11
  170.2 1.0 copy-start.5
  258.7 22.8 %collective-permute-start.5 = (f32[512,512]{0,1:T(8,128)S(1)}, f32[512,512]{0,1:T(8,128)S(1)}, u32[]{:S(2)}, u32[]{:S(2)}) collective-permute-start(f32[512,512]{0,1:T(8,128)S(1)} %fusion.24), channel_id=1, source_target_pairs={{0,32},{32,0},{64,96},{96,64},{128,160},{160,128},{192,224},{224,1... | collective-permute-start | bytes 3145736 | tf_op jit(solution)/shard_map/ppermute | solution.py:23
  286.1 1.0 copy-start.2
  375.2 50.2 %collective-permute-start.6 = (f32[512,512]{0,1:T(8,128)S(1)}, f32[512,512]{0,1:T(8,128)S(1)}, u32[]{:S(2)}, u32[]{:S(2)}) collective-permute-start(f32[512,512]{0,1:T(8,128)S(1)} %fusion.21), channel_id=1, source_target_pairs={{0,64},{64,0},{32,96},{96,32},{128,192},{192,128},{160,224},{224,1... | collective-permute-start | bytes 3145736 | tf_op jit(solution)/shard_map/ppermute | solution.py:23
  430.0 1.0 copy-start.3
  519.1 97.3 %collective-permute-start.7 = (f32[512,512]{0,1:T(8,128)S(1)}, f32[512,512]{0,1:T(8,128)S(1)}, u32[]{:S(2)}, u32[]{:S(2)}) collective-permute-start(f32[512,512]{0,1:T(8,128)S(1)} %fusion.18), channel_id=1, source_target_pairs={{0,128},{128,0},{32,160},{160,32},{64,192},{192,64},{96,224},{224,... | collective-permute-start | bytes 3145736 | tf_op jit(solution)/shard_map/ppermute | solution.py:23
  621.0 1.0 copy-start.4
  711.1 85.8 %collective-permute-start.8 = (f32[512,512]{0,1:T(8,128)}, f32[512,512]{0,1:T(8,128)}, u32[]{:S(2)}, u32[]{:S(2)}) collective-permute-start(f32[512,512]{0,1:T(8,128)} %fusion.15), channel_id=1, source_target_pairs={{0,256},{256,0},{32,288},{288,32},{64,320},{320,64},{96,352},{352,... | collective-permute-start | bytes 3145736 | tf_op jit(solution)/shard_map/ppermute | solution.py:23
  803.2 1.0 copy-start.1
